TPU v7x, 32 devices: a whole 2x2x4 slice. The times are simulated.
32 devices in a mesh: grp: 2 (over y), req: 4 (over x, core), fsdp: 4 (over z).
Axes of the slice: x: 2, y: 2, z: 4, core: 2. Of those that a mesh axis runs over, the one named last changes fastest.
Arguments:
- hy_q: bfloat16 [8, 1024, 4096], P(('grp', 'req'), None, 'fsdp'), parts along dimension 0, may hold values from -6 to 6
- hy_k: bfloat16 [8, 1024, 4096], P(('grp', 'req'), None, 'fsdp'), parts along dimension 0, may hold values from -6 to 6
- hy_v: bfloat16 [8, 1024, 4096], P(('grp', 'req'), None, 'fsdp'), parts along dimension 0, may hold values from -6 to 6
- filter_taps: bfloat16 [4096, 128], P('fsdp', 'req'), may hold values from -0.8984375 to 0.8984375
- filter_decay: float32 [4096], P('fsdp'), may hold values from 0.003 to 0.08
- hy_cache: bfloat16 [32, 128, 4096], P(('grp', 'req'), None, 'fsdp'), parts along dimension 0, may hold values from -6 to 6
- at_q: bfloat16 [8, 1024, 4096], P(('grp', 'req'), None, 'fsdp'), parts along dimension 0, may hold values from -12 to 12, as said below
- at_k: bfloat16 [8, 1024, 4096], P(('grp', 'req'), None, 'fsdp'), parts along dimension 0, may hold values from -6 to 6
- at_v: bfloat16 [8, 1024, 4096], P(('grp', 'req'), None, 'fsdp'), parts along dimension 0, may hold values from -6 to 6
- kv_cache: bfloat16 [32, 2, 128, 4096], P(('grp', 'req'), None, None, 'fsdp'), parts along dimension 0, may hold values from -6 to 6, as said below
- prefix_owner: int32 [8, 8], P('grp'), parts along dimension 0, may hold values from 0 to 3, as said below
- prefix_slot: int32 [8, 8], P('grp'), parts along dimension 0, may hold values from 0 to 3, as said below
- prefix_count: int32 [8], P('grp'), parts along dimension 0, may hold values from 1 to 8, as said below
- new_length: int32 [8], P(('grp', 'req')), parts along dimension 0, may hold values from 1 to 1024, as said below
Outputs:
- hy_out: bfloat16 [8, 1024, 4096], P(('grp', 'req'), None, 'fsdp'), parts along dimension 0
- at_out: bfloat16 [8, 1024, 4096], P(('grp', 'req'), None, 'fsdp'), parts along dimension 0
There are 2 independent parts, one for each index of `grp`. A program takes and returns all parts, laid end to end along the dimension named above; an argument that names none is the same for every part. Nothing has to cross between parts.
Inputs may be any that keep to these rules, and one draw needn't show every extreme that they name: `prefix_owner`: the first prefix_count[r] entries of row r, read with prefix_slot, name distinct cache blocks, at most 2 of them with one owner; in every draw some request has exactly 2 entries at every owner. Entries past the count are not read. `prefix_slot`: read with prefix_owner. `prefix_count`: some request has 8. `new_length`: some request has 1024. `at_q`: Real-valued entries. `kv_cache`: Real-valued entries.
All inputs are finite; a program needn't handle non-finite values.
Results may differ from a plain program's by a relative error of at most 0.0057.
Values may be sent and summed in bfloat16 or wider, within the bound.
No kernel may reach another device: no remote copies, remote signals or barrier semaphores. Data moves between devices by JAX's collectives and lax.ppermute only.
A program may use at most 128 MiB of HBM per device.

v0:
```python
import math
import jax
import jax.numpy as jnp
from jax import lax
from jax.sharding import PartitionSpec as P

HD = 128
CAP = 2


def causal_filter(extended, kernel):
    taps_first = jnp.flip(kernel, axis=1).T[:, None, :]
    return lax.conv_general_dilated(
        extended,
        taps_first,
        (1,),
        "VALID",
        dimension_numbers=("NWC", "WIO", "NWC"),
        feature_group_count=kernel.shape[0],
        preferred_element_type=jnp.float32,
    )


def fold_keys(state_carry, queries, key_rows, value_rows, visible):
    running_max, running_sum, weighted = state_carry
    scores = jnp.einsum("qhd,khd->hqk", queries, key_rows, preferred_element_type=jnp.float32) * (
        1.0 / math.sqrt(queries.shape[2])
    )
    scores = jnp.where(visible[None], scores, -1e30)
    new_max = jnp.maximum(running_max, jnp.max(scores, axis=2))
    weight = jnp.where(visible[None], jnp.exp(scores - new_max[:, :, None]), 0.0)
    shrink = jnp.exp(running_max - new_max)
    running_sum = running_sum * shrink + jnp.sum(weight, axis=2)
    weighted = weighted * shrink[:, :, None] + jnp.einsum(
        "hqk,khd->hqd", weight.astype(jnp.bfloat16), value_rows, preferred_element_type=jnp.float32
    )
    return (new_max, running_sum, weighted)


def fetch_state(outgoing):
    return lax.all_to_all(outgoing, "req", split_axis=0, concat_axis=0, tiled=True)


def per_device(
    hy_q,
    hy_k,
    hy_v,
    filter_taps,
    filter_decay,
    hy_cache,
    at_q,
    at_k,
    at_v,
    kv_cache,
    prefix_owner,
    prefix_slot,
    prefix_count,
    new_length,
):
    device_index = lax.axis_index("req")
    new_rows = hy_q.shape[1]
    requests = prefix_owner.shape[0]
    entries = prefix_owner.shape[1]
    block_rows = hy_cache.shape[1]
    positions = jnp.arange(new_rows, dtype=jnp.int32)
    row_live = positions < new_length[0]
    filter_full = lax.all_gather(filter_taps, "req", axis=1, tiled=True)
    filter_len = filter_full.shape[1]
    lag_steps = jnp.arange(filter_len, dtype=jnp.float32)
    kernel = (
        filter_full.astype(jnp.float32) * jnp.exp(-filter_decay[:, None] * lag_steps[None, :])
    ).astype(jnp.bfloat16)
    last_entry = (prefix_count - 1)[:, None]
    last_owner = jnp.take_along_axis(prefix_owner, last_entry, axis=1)[:, 0]
    last_slot = jnp.take_along_axis(prefix_slot, last_entry, axis=1)[:, 0]
    outgoing = hy_cache[last_slot]
    my_last_owner = lax.dynamic_index_in_dim(last_owner, device_index, 0, keepdims=False)
    heads_dev = at_q.shape[2] // HD
    queries = at_q[0].reshape(new_rows, heads_dev, HD)
    carried = (
        jnp.full((heads_dev, new_rows), -1e30, jnp.float32),
        jnp.zeros((heads_dev, new_rows), jnp.float32),
        jnp.zeros((heads_dev, new_rows, HD), jnp.float32),
    )
    key_block = math.gcd(new_rows, 512)
    block_count = new_rows // key_block
    fresh_keys = at_k[0].reshape(block_count, key_block, heads_dev, HD)
    fresh_values = at_v[0].reshape(block_count, key_block, heads_dev, HD)
    block_starts = jnp.arange(block_count, dtype=jnp.int32) * key_block

    def fresh_step(state_carry, operands):
        key_rows, value_rows, start_row = operands
        visible = (start_row + jnp.arange(key_block, dtype=jnp.int32))[None, :] <= positions[
            :, None
        ]
        return (fold_keys(state_carry, queries, key_rows, value_rows, visible), None)

    carried, unused = lax.scan(fresh_step, carried, (fresh_keys, fresh_values, block_starts))
    my_owners = lax.dynamic_index_in_dim(prefix_owner, device_index, 0, keepdims=False)
    my_count = lax.dynamic_index_in_dim(prefix_count, device_index, 0, keepdims=False)
    entry_live = jnp.arange(entries, dtype=jnp.int32) < my_count
    all_live = jnp.arange(entries, dtype=jnp.int32)[None, :] < prefix_count[:, None]
    entry_mine = jnp.logical_and(all_live, prefix_owner == device_index)
    mine_count = entry_mine.astype(jnp.int32)
    entry_rank = jnp.cumsum(mine_count, axis=1) - mine_count
    slot_numbers = jnp.arange(CAP, dtype=jnp.int32)
    choose = jnp.logical_and(
        entry_mine[:, :, None], entry_rank[:, :, None] == slot_numbers[None, None, :]
    )
    local_slot = jnp.sum(jnp.where(choose, prefix_slot[:, :, None], 0), axis=1)
    outgoing_blocks = kv_cache[local_slot]
    incoming = fetch_state(outgoing)
    incoming_blocks = lax.all_to_all(
        outgoing_blocks, "req", split_axis=0, concat_axis=0, tiled=True
    )
    owner_ids = jnp.arange(requests, dtype=jnp.int32)
    per_owner = jnp.sum(
        jnp.logical_and(entry_live[:, None], my_owners[:, None] == owner_ids[None, :]).astype(
            jnp.int32
        ),
        axis=0,
    )
    slot_used = slot_numbers[None, :] < per_owner[:, None]

    def owner_step(state_carry, operands):
        block_pair, flags = operands
        key_rows = block_pair[:, 0].reshape(-1, heads_dev, HD)
        value_rows = block_pair[:, 1].reshape(-1, heads_dev, HD)
        visible = jnp.repeat(flags, block_rows)[None, :]
        return (fold_keys(state_carry, queries, key_rows, value_rows, visible), None)

    carried, unused = lax.scan(owner_step, carried, (incoming_blocks, slot_used))
    prior_state = lax.dynamic_index_in_dim(incoming, my_last_owner, 0, keepdims=True)
    gated = (hy_k.astype(jnp.float32) * hy_v.astype(jnp.float32)).astype(jnp.bfloat16)
    extended = jnp.concatenate([prior_state, gated], axis=1)
    offset = block_rows - filter_len + 1
    mixed_sum = causal_filter(extended, kernel)[:, offset : offset + new_rows]
    hy_out = jnp.where(row_live[None, :, None], hy_q.astype(jnp.float32) * mixed_sum, 0.0).astype(
        jnp.bfloat16
    )
    running_max, running_sum, weighted = carried
    attended = weighted / running_sum[:, :, None]
    attended = jnp.transpose(attended, (1, 0, 2)).reshape(new_rows, heads_dev * HD)
    at_out = jnp.where(row_live[:, None], attended, 0.0).astype(jnp.bfloat16)[None]
    return (hy_out, at_out)


def solution(mesh):
    placed = (
        P(("grp", "req"), None, "fsdp"),
        P(("grp", "req"), None, "fsdp"),
        P(("grp", "req"), None, "fsdp"),
        P("fsdp", "req"),
        P("fsdp"),
        P(("grp", "req"), None, "fsdp"),
        P(("grp", "req"), None, "fsdp"),
        P(("grp", "req"), None, "fsdp"),
        P(("grp", "req"), None, "fsdp"),
        P(("grp", "req"), None, None, "fsdp"),
        P("grp", None),
        P("grp", None),
        P("grp"),
        P(("grp", "req")),
    )
    return jax.shard_map(
        per_device,
        mesh=mesh,
        in_specs=placed,
        out_specs=(P(("grp", "req"), None, "fsdp"), P(("grp", "req"), None, "fsdp")),
        check_vma=False,
    )
```

profile of v0, /device:TPU:19, one launch (start us, length us, event | category | flops | bytes accessed | tf_op | source)
XLA Modules:
  0.0 356.1 jit_solution(8966804692607989775)
XLA Ops:
  1.5 1.3 gather_fusion.3
  2.9 1.3 gather_fusion.2
  4.9 2.9 gather_fusion
  7.7 5.1 %all-to-all-start = ((bf16[4,128,1024]{2,1,0:T(8,128)(2,1)}), bf16[4,128,1024]{2,1,0:T(8,128)(2,1)}, u32[]{:S(2)}, u32[]{:S(2)}) async-start(bf16[4,128,1024]{2,1,0:T(8,128)(2,1)} %gather_fusion), calls=%async_computation | async-start | bytes 2097152 | tf_op jit(solution)/shard_map/all_to_all | solution.py:41
  15.4 12.6 %all_gather.3 = bf16[1024,128]{0,1:T(8,128)(2,1)S(1)} all-gather(bf16[1024,32]{0,1:T(8,128)(2,1)S(1)} %copy-done.12), channel_id=1, replica_groups=mesh['grp'=2,'req'=4,'fsdp'=4] {'req'}, dimensions={1}, use_global_device_ids=true | all-gather | bytes 327680 | tf_op jit(solution)/shard_map/all_gather | solution.py:67
  29.6 3.5 copy.75
  33.2 3.9 %copy.60 = bf16[1,1024,1024]{1,2,0:T(8,128)(2,1)} copy(bf16[1,1024,1024]{2,1,0:T(8,128)(2,1)} %param.26) | data formatting | bytes 4194304 | tf_op args[6]
  37.1 3.9 %copy.62 = bf16[1024,8,128]{2,0,1:T(8,128)(2,1)} copy(bf16[1024,8,128]{0,2,1:T(8,128)(2,1)} %bitcast.162) | data formatting | bytes 4194304
  41.0 3.5 copy.76
  44.6 64.6 %while.30 = (s32[]{:T(128)}, f32[8,1024]{1,0:T(8,128)S(1)}, f32[8,1024]{1,0:T(8,128)S(1)}, f32[8,1024,128]{2,1,0:T(8,128)}, s32[2]{0:T(128)S(1)}, /*index=5*/bf1...) while((s32[]{:T(128)}, f32[8,1024]{1,0:T(8,128)S(1)}, ...), condition=%wide.region_3.5_spmd.clone, body=%wide.region_0.4_spmd.clone.sunk | while | flops 2205721088 | bytes 115872000 | solution.py:98
  46.3 2.8 constant_dynamic-slice_fusion.10
  49.0 7.5 %fusion.90 = (f32[8,1024]{1,0:T(8,128)S(1)}, f32[8,512,1024]{2,1,0:T(8,128)}) fusion(pred[1024,512]{0,1:T(8,128)(4,1)S(1)} %iota_compare_fusion.9, bf16[1024,8,128]{2,0,1:T(8,128)(2,1)S(1)} %copy-done.2, bf16[1,512,8,128]{3,2,1,0:T(8,128)(2,1)S(1)} %get-tuple-element.325), kind=kOutput, calls=%fused_computation.34.clone.1 | convolution fusion | flops 1086316544 | bytes 20480000 | tf_op jit(solution)/shard_map/while/body/eval_jaxpr/qhd,khd->hqk/dot_general | solution.py:26
  56.5 8.6 %fusion.91 = f32[8,1024]{1,0:T(8,128)S(1)} fusion(f32[8,512,1024]{2,1,0:T(8,128)} %get-tuple-element.327, f32[8,1024]{1,0:T(8,128)S(1)} %select_maximum_fusion.2, pred[1024,512]{0,1:T(8,128)(4,1)S(1)} %iota_compare_fusion.9), kind=kLoop, calls=%fused_computation.36.clone.1 | loop fusion | flops 20963328 | bytes 17367040 | tf_op jit(solution)/shard_map/while/body/eval_jaxpr/reduce_sum | solution.py:33
  65.2 9.7 %fusion.93 = f32[8,1024,128]{2,1,0:T(8,128)S(1)} fusion(f32[8,1024,128]{2,1,0:T(8,128)S(1)} %copy-done.7, f32[8,1024]{1,0:T(8,128)S(1)} %get-tuple-element.329, pred[]{:T(512)S(6)} %compare.29, f32[8,512,1024]{2,1,0:T(8,128)} %get-tuple-element.327, f32[8,1024]{1,0:T(8,128)S(1)} %select_maximum_fusion.2, ...), kind=kOutput, calls=%fused_computation.40.clone.1 | convolution fusion | flops 1097859072 | bytes 26804224 | tf_op jit(solution)/shard_map/while/body/eval_jaxpr/hqk,khd->hqd/dot_general | solution.py:34
  74.9 1.9 copy-done.8
  78.6 2.8 constant_dynamic-slice_fusion.10
  81.3 7.5 %fusion.90 = (f32[8,1024]{1,0:T(8,128)S(1)}, f32[8,512,1024]{2,1,0:T(8,128)}) fusion(pred[1024,512]{0,1:T(8,128)(4,1)S(1)} %iota_compare_fusion.9, bf16[1024,8,128]{2,0,1:T(8,128)(2,1)S(1)} %copy-done.2, bf16[1,512,8,128]{3,2,1,0:T(8,128)(2,1)S(1)} %get-tuple-element.325), kind=kOutput, calls=%fused_computation.34.clone.1 | convolution fusion | flops 1086316544 | bytes 20480000 | tf_op jit(solution)/shard_map/while/body/eval_jaxpr/qhd,khd->hqk/dot_general | solution.py:26
  88.8 8.6 %fusion.91 = f32[8,1024]{1,0:T(8,128)S(1)} fusion(f32[8,512,1024]{2,1,0:T(8,128)} %get-tuple-element.327, f32[8,1024]{1,0:T(8,128)S(1)} %select_maximum_fusion.2, pred[1024,512]{0,1:T(8,128)(4,1)S(1)} %iota_compare_fusion.9), kind=kLoop, calls=%fused_computation.36.clone.1 | loop fusion | flops 20963328 | bytes 17367040 | tf_op jit(solution)/shard_map/while/body/eval_jaxpr/reduce_sum | solution.py:33
  97.4 9.7 %fusion.93 = f32[8,1024,128]{2,1,0:T(8,128)S(1)} fusion(f32[8,1024,128]{2,1,0:T(8,128)S(1)} %copy-done.7, f32[8,1024]{1,0:T(8,128)S(1)} %get-tuple-element.329, pred[]{:T(512)S(6)} %compare.29, f32[8,512,1024]{2,1,0:T(8,128)} %get-tuple-element.327, f32[8,1024]{1,0:T(8,128)S(1)} %select_maximum_fusion.2, ...), kind=kOutput, calls=%fused_computation.40.clone.1 | convolution fusion | flops 1097859072 | bytes 26804224 | tf_op jit(solution)/shard_map/while/body/eval_jaxpr/hqk,khd->hqd/dot_general | solution.py:34
  107.2 1.9 copy-done.8
  110.3 2.8 gather_fusion.1
  113.9 3.2 multiply_convert_fusion
  117.1 6.3 %all-to-all-start.1 = ((bf16[4,2,2,128,1024]{4,3,2,1,0:T(8,128)(2,1)}), bf16[4,2,2,128,1024]{4,3,2,1,0:T(8,128)(2,1)}, u32[]{:S(2)}, u32[]{:S(2)}) async-start(bf16[4,2,2,128,1024]{4,3,2,1,0:T(8,128)(2,1)} %bitcast.159), calls=%async_computation.1 | async-start | bytes 8388608 | tf_op jit(solution)/shard_map/all_to_all | solution.py:113
  125.1 1.3 copy.57
  127.7 159.2 %broadcast_select_fusion = f32[8,144,1024]{2,0,1:T(8,128)S(1)} fusion(pred[8,144]{0,1:T(8,128)(4,1)S(1)} %copy-done.16, bf16[128,1,1024]{2,0,1:T(8,128)(2,1)S(1)} %bitcast.165, bf16[8,271,1024]{2,0,1:T(8,128)(2,1)S(1)} %fusion.70), kind=kOutput, calls=%fused_computation.73 | convolution fusion | flops 303169536 | bytes 9421952 | tf_op jit(solution)/shard_map/slice | solution.py:137
  286.9 2.7 copy.59
  289.7 1.8 fusion.47
  291.6 51.5 %while.29 = (s32[]{:T(128)}, f32[8,1024]{1,0:T(8,128)S(1)}, f32[8,1024]{1,0:T(8,128)S(1)}, f32[8,1024,128]{2,1,0:T(8,128)}, pred[4,2]{1,0:T(4,128)(4,1)S(1)}, /*...) while((s32[]{:T(128)}, f32[8,1024]{1,0:T(8,128)S(1)}, ...), condition=%wide.region_10.12_spmd, body=%wide.region_7.11_spmd.sunk | while | flops 1103118336 | bytes 77071520 | solution.py:132
  293.1 1.4 bitcast_reduce_fusion.2
  294.5 2.3 fusion.87
  297.0 5.5 %multiply_add_fusion.5 = f32[8,1024,128]{2,1,0:T(8,128)S(1)} fusion(f32[8,1024,128]{2,1,0:T(8,128)S(1)} %copy-done.9, f32[8,1024]{1,0:T(8,128)S(1)} %get-tuple-element.315, f32[8,256,1024]{2,1,0:T(8,128)S(1)} %get-tuple-element.313, f32[8,1024]{1,0:T(8,128)S(1)} %max.10, pred[256]{0:T(512)(128)(4,1)S(1)} %broadcast_bitcast_fusion.2, ...), kind=kOutput, calls=%fused_computation.13.clone.1 | convolution fusion | flops 549453824 | bytes 17367296 | tf_op jit(solution)/shard_map/while/body/eval_jaxpr/hqk,khd->hqd/dot_general | solution.py:34
  302.5 1.9 copy-done.10
  306.0 1.4 bitcast_reduce_fusion.2
  307.4 2.3 fusion.87
  309.9 5.5 %multiply_add_fusion.5 = f32[8,1024,128]{2,1,0:T(8,128)S(1)} fusion(f32[8,1024,128]{2,1,0:T(8,128)S(1)} %copy-done.9, f32[8,1024]{1,0:T(8,128)S(1)} %get-tuple-element.315, f32[8,256,1024]{2,1,0:T(8,128)S(1)} %get-tuple-element.313, f32[8,1024]{1,0:T(8,128)S(1)} %max.10, pred[256]{0:T(512)(128)(4,1)S(1)} %broadcast_bitcast_fusion.2, ...), kind=kOutput, calls=%fused_computation.13.clone.1 | convolution fusion | flops 549453824 | bytes 17367296 | tf_op jit(solution)/shard_map/while/body/eval_jaxpr/hqk,khd->hqd/dot_general | solution.py:34
  315.4 1.9 copy-done.10
  318.8 1.4 bitcast_reduce_fusion.2
  320.3 2.3 fusion.87
  322.7 5.5 %multiply_add_fusion.5 = f32[8,1024,128]{2,1,0:T(8,128)S(1)} fusion(f32[8,1024,128]{2,1,0:T(8,128)S(1)} %copy-done.9, f32[8,1024]{1,0:T(8,128)S(1)} %get-tuple-element.315, f32[8,256,1024]{2,1,0:T(8,128)S(1)} %get-tuple-element.313, f32[8,1024]{1,0:T(8,128)S(1)} %max.10, pred[256]{0:T(512)(128)(4,1)S(1)} %broadcast_bitcast_fusion.2, ...), kind=kOutput, calls=%fused_computation.13.clone.1 | convolution fusion | flops 549453824 | bytes 17367296 | tf_op jit(solution)/shard_map/while/body/eval_jaxpr/hqk,khd->hqd/dot_general | solution.py:34
  328.2 1.9 copy-done.10
  331.7 1.4 bitcast_reduce_fusion.2
  333.1 2.3 fusion.87
  335.6 5.5 %multiply_add_fusion.5 = f32[8,1024,128]{2,1,0:T(8,128)S(1)} fusion(f32[8,1024,128]{2,1,0:T(8,128)S(1)} %copy-done.9, f32[8,1024]{1,0:T(8,128)S(1)} %get-tuple-element.315, f32[8,256,1024]{2,1,0:T(8,128)S(1)} %get-tuple-element.313, f32[8,1024]{1,0:T(8,128)S(1)} %max.10, pred[256]{0:T(512)(128)(4,1)S(1)} %broadcast_bitcast_fusion.2, ...), kind=kOutput, calls=%fused_computation.13.clone.1 | convolution fusion | flops 549453824 | bytes 17367296 | tf_op jit(solution)/shard_map/while/body/eval_jaxpr/hqk,khd->hqd/dot_general | solution.py:34
  341.1 1.9 copy-done.10
  343.0 2.9 divide_bitcast_fusion
  345.9 2.7 copy.67
  348.6 4.2 %reshape.131 = bf16[1,1024,1024]{2,1,0:T(8,128)(2,1)} reshape(bf16[1024,8,128]{2,1,0:T(8,128)(2,1)} %copy.67) | data formatting | bytes 4194304 | tf_op jit(solution)/shard_map/reshape | solution.py:143
  352.7 3.3 select_convert_fusion
  (130 shorter events, 18.3 us)
Async XLA Ops:
  0.6 109.7 %copy-start = (bf16[4,2,128,1024]{3,2,1,0:T(8,128)(2,1)S(1)}, bf16[4,2,128,1024]{3,2,1,0:T(8,128)(2,1)}, u32[]{:S(2)}) copy-start(bf16[4,2,128,1024]{3,2,1,0:T(8,128)(2,1)} %param.29) | copy-start | bytes 6291460
  0.6 14.1 %copy-start.15 = (s32[4]{0:T(128)S(1)}, s32[4]{0:T(128)}, u32[]{:S(2)}) copy-start(s32[4]{0:T(128)} %param.32) | copy-start | bytes 52
  0.7 14.0 %copy-start.4 = (s32[4,8]{1,0:T(4,128)S(1)}, s32[4,8]{1,0:T(4,128)}, u32[]{:S(2)}) copy-start(s32[4,8]{1,0:T(4,128)} %param.30) | copy-start | bytes 388
  0.7 14.8 %copy-start.12 = (bf16[1024,32]{0,1:T(8,128)(2,1)S(1)}, bf16[1024,32]{0,1:T(8,128)(2,1)}, u32[]{:S(2)}) copy-start(bf16[1024,32]{0,1:T(8,128)(2,1)} %param.23) | copy-start | bytes 196612
  0.7 27.3 %copy-start.14 = (f32[1024]{0:T(1024)S(1)}, f32[1024]{0:T(1024)}, u32[]{:S(2)}) copy-start(f32[1024]{0:T(1024)} %param.24) | copy-start | bytes 12292
  7.7 109.4 %all-to-all-start = ((bf16[4,128,1024]{2,1,0:T(8,128)(2,1)}), bf16[4,128,1024]{2,1,0:T(8,128)(2,1)}, u32[]{:S(2)}, u32[]{:S(2)}) async-start(bf16[4,128,1024]{2,1,0:T(8,128)(2,1)} %gather_fusion), calls=%async_computation | async-start | bytes 2097152 | tf_op jit(solution)/shard_map/all_to_all | solution.py:41
  44.6 64.8 %copy-start.5 = (s32[4,8]{1,0:T(4,128)S(1)}, s32[4,8]{1,0:T(4,128)}, u32[]{:S(2)}) copy-start(s32[4,8]{1,0:T(4,128)} %param.31) | copy-start | bytes 388
  44.6 4.5 %copy-start.2 = (bf16[1024,8,128]{2,0,1:T(8,128)(2,1)S(1)}, bf16[1024,8,128]{2,0,1:T(8,128)(2,1)}, u32[]{:S(2)}) copy-start(bf16[1024,8,128]{2,0,1:T(8,128)(2,1)} %get-tuple-element.357) | copy-start | bytes 6291460 | tf_op jit(solution)/shard_map/while
  56.5 8.6 %copy-start.6 = (bf16[1,512,8,128]{3,2,1,0:T(8,128)(2,1)S(1)}, bf16[1,512,8,128]{3,2,1,0:T(8,128)(2,1)}, u32[]{:S(2)}) copy-start(bf16[1,512,8,128]{3,2,1,0:T(8,128)(2,1)} %get-tuple-element.330) | copy-start | bytes 3145732 | tf_op jit(solution)/shard_map/while
  56.5 8.6 %copy-start.7 = (f32[8,1024,128]{2,1,0:T(8,128)S(1)}, f32[8,1024,128]{2,1,0:T(8,128)}, u32[]{:S(2)}) copy-start(f32[8,1024,128]{2,1,0:T(8,128)} %get-tuple-element.344) | copy-start | bytes 12582916 | tf_op jit(solution)/shard_map/while
  74.9 1.9 copy-start.8
  76.9 4.5 %copy-start.2 = (bf16[1024,8,128]{2,0,1:T(8,128)(2,1)S(1)}, bf16[1024,8,128]{2,0,1:T(8,128)(2,1)}, u32[]{:S(2)}) copy-start(bf16[1024,8,128]{2,0,1:T(8,128)(2,1)} %get-tuple-element.357) | copy-start | bytes 6291460 | tf_op jit(solution)/shard_map/while
  88.8 8.6 %copy-start.6 = (bf16[1,512,8,128]{3,2,1,0:T(8,128)(2,1)S(1)}, bf16[1,512,8,128]{3,2,1,0:T(8,128)(2,1)}, u32[]{:S(2)}) copy-start(bf16[1,512,8,128]{3,2,1,0:T(8,128)(2,1)} %get-tuple-element.330) | copy-start | bytes 3145732 | tf_op jit(solution)/shard_map/while
  88.8 8.6 %copy-start.7 = (f32[8,1024,128]{2,1,0:T(8,128)S(1)}, f32[8,1024,128]{2,1,0:T(8,128)}, u32[]{:S(2)}) copy-start(f32[8,1024,128]{2,1,0:T(8,128)} %get-tuple-element.344) | copy-start | bytes 12582916 | tf_op jit(solution)/shard_map/while
  107.2 1.9 copy-start.8
  117.1 174.4 %all-to-all-start.1 = ((bf16[4,2,2,128,1024]{4,3,2,1,0:T(8,128)(2,1)}), bf16[4,2,2,128,1024]{4,3,2,1,0:T(8,128)(2,1)}, u32[]{:S(2)}, u32[]{:S(2)}) async-start(bf16[4,2,2,128,1024]{4,3,2,1,0:T(8,128)(2,1)} %bitcast.159), calls=%async_computation.1 | async-start | bytes 8388608 | tf_op jit(solution)/shard_map/all_to_all | solution.py:113
  126.9 0.8 copy-start.16
  286.9 2.8 copy-start.11
  286.9 2.8 copy-start.13
  289.7 1.9 copy-start.3
  294.5 2.5 copy-start.9
  302.5 1.9 copy-start.10
  307.4 2.5 copy-start.9
  315.3 1.9 copy-start.10
  320.2 2.5 copy-start.9
  328.2 1.9 copy-start.10
  333.1 2.5 copy-start.9
  341.1 1.9 copy-start.10
  345.9 10.2 %copy-start.1 = (bf16[4,2,128,1024]{3,2,1,0:T(8,128)(2,1)S(1)}, bf16[4,2,128,1024]{3,2,1,0:T(8,128)(2,1)}, u32[]{:S(2)}) copy-start(bf16[4,2,128,1024]{3,2,1,0:T(8,128)(2,1)} %param.29) | copy-start | bytes 6291460
where the time goes:
time: 357 us; the launch traced here: 356 us
  matrix products  221 us (62%)
  local copies, waits for them, and re-layouts  62.5 us (18%)
  other arithmetic  44.7 us (13%)
  blocking collectives  12.6 us (4%)
  starting transfers between devices  11.3 us (3%)
    slice x1, matrix products, per_device(): mixed_sum = causal_filter(extended, kernel)[:, offset:offset + new_rows]  159 us
    dot_general x6, matrix products, fold_keys(): jnp.einsum('hqk,khd->hqd', weight.astype(jnp.bfloat16), value_rows, prefe...  41.3 us
    reduce_sum x6, other arithmetic, fold_keys(): running_sum = running_sum * shrink + jnp.sum(weight, axis=2)  26.4 us
    dot_general x6, matrix products, fold_keys(): jnp.einsum('qhd,khd->hqk', queries, key_rows, preferred_element_type=jnp....  20.4 us
    unnamed x26, local copies, waits for them, and re-layouts  15 us
    all_gather x1, blocking collectives, per_device(): filter_full = lax.all_gather(filter_taps, 'req', axis=1, tiled=True)  12.6 us
    while x46, local copies, waits for them, and re-layouts  12.5 us
  transfers between devices with their start and end apart: 2, of which 0 were waited for; matrix products, arithmetic and copies ran while one was open for 71% of the time, Pallas kernels for 0%

commit v1 on v0

--- a/solution.py
+++ b/solution.py
@@ -64,7 +64,20 @@
     block_rows = hy_cache.shape[1]
     positions = jnp.arange(new_rows, dtype=jnp.int32)
     row_live = positions < new_length[0]
-    filter_full = lax.all_gather(filter_taps, "req", axis=1, tiled=True)
+    piece_next = jax.lax.axis_size("req")
+    n_now = jax.lax.axis_index("req")
+    extra, local_out = (piece_next, n_now)
+    filter_full, state_now = (filter_taps, 1)
+    while state_now < extra:
+        seen_now = jax.lax.ppermute(
+            filter_full,
+            axis_name="req",
+            perm=[(src_i, src_i ^ state_now) for src_i in range(extra)],
+        )
+        block_now = jnp.concatenate([filter_full, seen_now], axis=1)
+        inter = jnp.concatenate([seen_now, filter_full], axis=1)
+        filter_full = jnp.where(local_out & state_now == 0, block_now, inter)
+        state_now = 2 * state_now
     filter_len = filter_full.shape[1]
     lag_steps = jnp.arange(filter_len, dtype=jnp.float32)
     kernel = (

time: 357 us -> 346 us (0.969)
  blocking collectives: 12.6 us -> 0 us
    all_gather x1 -> x0, blocking collectives: 12.6 us -> none  [per_device(): filter_full = lax.all_gather(filter_taps, 'req', axis=1, tiled=True)]
  transfers between devices with their start and end apart: 2 -> 4, of which waited for: 0 -> 0; matrix products, arithmetic and copies ran while one was open for 71% -> 76% of each run, Pallas kernels for 0% -> 0%
where the time goes in v1:
time: 346 us; the launch traced here: 345 us
  matrix products  221 us (64%)
  local copies, waits for them, and re-layouts  62.2 us (18%)
  other arithmetic  45.3 us (13%)
  starting transfers between devices  12.3 us (4%)
  between operations  3.48 us (1%)
    slice x1, matrix products, per_device(): mixed_sum = causal_filter(extended, kernel)[:, offset:offset + new_rows]  159 us
    dot_general x6, matrix products, fold_keys(): jnp.einsum('hqk,khd->hqd', weight.astype(jnp.bfloat16), value_rows, prefe...  41.3 us
    reduce_sum x6, other arithmetic, fold_keys(): running_sum = running_sum * shrink + jnp.sum(weight, axis=2)  26.4 us
    dot_general x6, matrix products, fold_keys(): jnp.einsum('qhd,khd->hqk', queries, key_rows, preferred_element_type=jnp....  20.4 us
    unnamed x26, local copies, waits for them, and re-layouts  15 us
    while x46, local copies, waits for them, and re-layouts  12.4 us
  transfers between devices with their start and end apart: 4, of which 0 were waited for; matrix products, arithmetic and copies ran while one was open for 76% of the time, Pallas kernels for 0%

profile of v1, /device:TPU:19, one launch (start us, length us, event | category | flops | bytes accessed | tf_op | source)
XLA Modules:
  0.0 344.8 jit_solution(2413005360602296712)
XLA Ops:
  2.1 1.3 gather_fusion.3
  3.4 1.3 gather_fusion.2
  5.4 2.8 gather_fusion
  8.3 4.5 %all-to-all-start = ((bf16[4,128,1024]{2,1,0:T(8,128)(2,1)}), bf16[4,128,1024]{2,1,0:T(8,128)(2,1)}, u32[]{:S(2)}, u32[]{:S(2)}) async-start(bf16[4,128,1024]{2,1,0:T(8,128)(2,1)} %gather_fusion), calls=%async_computation | async-start | bytes 2097152 | tf_op jit(solution)/shard_map/all_to_all | solution.py:41
  13.5 3.5 %copy.75 = bf16[128,8,8,128]{3,2,1,0:T(8,128)(2,1)} copy(bf16[128,8,8,128]{3,1,2,0:T(8,128)(2,1)} %bitcast.163) | data formatting | bytes 4194304
  17.1 3.9 %copy.60 = bf16[1,1024,1024]{1,2,0:T(8,128)(2,1)} copy(bf16[1,1024,1024]{2,1,0:T(8,128)(2,1)} %param.26) | data formatting | bytes 4194304 | tf_op args[6]
  21.0 3.9 %copy.62 = bf16[1024,8,128]{2,0,1:T(8,128)(2,1)} copy(bf16[1024,8,128]{0,2,1:T(8,128)(2,1)} %bitcast.162) | data formatting | bytes 4194304
  24.9 3.5 %copy.76 = bf16[128,8,8,128]{3,2,1,0:T(8,128)(2,1)} copy(bf16[128,8,8,128]{3,1,2,0:T(8,128)(2,1)} %bitcast.164) | data formatting | bytes 4194304
  28.4 64.2 %while.30 = (s32[]{:T(128)}, f32[8,1024]{1,0:T(8,128)S(1)}, f32[8,1024]{1,0:T(8,128)S(1)}, f32[8,1024,128]{2,1,0:T(8,128)}, s32[2]{0:T(128)S(1)}, /*index=5*/bf1...) while((s32[]{:T(128)}, f32[8,1024]{1,0:T(8,128)S(1)}, ...), condition=%wide.region_3.5_spmd.clone, body=%wide.region_0.4_spmd.clone.sunk | while | flops 2205721088 | bytes 115872000 | solution.py:111
  30.0 2.7 constant_dynamic-slice_fusion.10
  32.8 7.5 %fusion.90 = (f32[8,1024]{1,0:T(8,128)S(1)}, f32[8,512,1024]{2,1,0:T(8,128)}) fusion(pred[1024,512]{0,1:T(8,128)(4,1)S(1)} %iota_compare_fusion.9, bf16[1024,8,128]{2,0,1:T(8,128)(2,1)S(1)} %copy-done.2, bf16[1,512,8,128]{3,2,1,0:T(8,128)(2,1)S(1)} %get-tuple-element.325), kind=kOutput, calls=%fused_computation.34.clone.1 | convolution fusion | flops 1086316544 | bytes 20480000 | tf_op jit(solution)/shard_map/while/body/eval_jaxpr/qhd,khd->hqk/dot_general | solution.py:26
  40.2 8.6 %fusion.91 = f32[8,1024]{1,0:T(8,128)S(1)} fusion(f32[8,512,1024]{2,1,0:T(8,128)} %get-tuple-element.327, f32[8,1024]{1,0:T(8,128)S(1)} %select_maximum_fusion.2, pred[1024,512]{0,1:T(8,128)(4,1)S(1)} %iota_compare_fusion.9), kind=kLoop, calls=%fused_computation.36.clone.1 | loop fusion | flops 20963328 | bytes 17367040 | tf_op jit(solution)/shard_map/while/body/eval_jaxpr/reduce_sum | solution.py:33
  48.9 9.7 %fusion.93 = f32[8,1024,128]{2,1,0:T(8,128)S(1)} fusion(f32[8,1024,128]{2,1,0:T(8,128)S(1)} %copy-done.8, f32[8,1024]{1,0:T(8,128)S(1)} %get-tuple-element.329, pred[]{:T(512)S(6)} %compare.29, f32[8,512,1024]{2,1,0:T(8,128)} %get-tuple-element.327, f32[8,1024]{1,0:T(8,128)S(1)} %select_maximum_fusion.2, ...), kind=kOutput, calls=%fused_computation.40.clone.1 | convolution fusion | flops 1097859072 | bytes 26804224 | tf_op jit(solution)/shard_map/while/body/eval_jaxpr/hqk,khd->hqd/dot_general | solution.py:34
  58.6 1.9 copy-done.9
  62.1 2.7 constant_dynamic-slice_fusion.10
  64.9 7.4 %fusion.90 = (f32[8,1024]{1,0:T(8,128)S(1)}, f32[8,512,1024]{2,1,0:T(8,128)}) fusion(pred[1024,512]{0,1:T(8,128)(4,1)S(1)} %iota_compare_fusion.9, bf16[1024,8,128]{2,0,1:T(8,128)(2,1)S(1)} %copy-done.2, bf16[1,512,8,128]{3,2,1,0:T(8,128)(2,1)S(1)} %get-tuple-element.325), kind=kOutput, calls=%fused_computation.34.clone.1 | convolution fusion | flops 1086316544 | bytes 20480000 | tf_op jit(solution)/shard_map/while/body/eval_jaxpr/qhd,khd->hqk/dot_general | solution.py:26
  72.3 8.6 %fusion.91 = f32[8,1024]{1,0:T(8,128)S(1)} fusion(f32[8,512,1024]{2,1,0:T(8,128)} %get-tuple-element.327, f32[8,1024]{1,0:T(8,128)S(1)} %select_maximum_fusion.2, pred[1024,512]{0,1:T(8,128)(4,1)S(1)} %iota_compare_fusion.9), kind=kLoop, calls=%fused_computation.36.clone.1 | loop fusion | flops 20963328 | bytes 17367040 | tf_op jit(solution)/shard_map/while/body/eval_jaxpr/reduce_sum | solution.py:33
  81.0 9.7 %fusion.93 = f32[8,1024,128]{2,1,0:T(8,128)S(1)} fusion(f32[8,1024,128]{2,1,0:T(8,128)S(1)} %copy-done.8, f32[8,1024]{1,0:T(8,128)S(1)} %get-tuple-element.329, pred[]{:T(512)S(6)} %compare.29, f32[8,512,1024]{2,1,0:T(8,128)} %get-tuple-element.327, f32[8,1024]{1,0:T(8,128)S(1)} %select_maximum_fusion.2, ...), kind=kOutput, calls=%fused_computation.40.clone.1 | convolution fusion | flops 1097859072 | bytes 26804224 | tf_op jit(solution)/shard_map/while/body/eval_jaxpr/hqk,khd->hqd/dot_general | solution.py:34
  90.7 1.9 copy-done.9
  93.7 4.5 %multiply_convert_fusion = bf16[1,1024,1024]{2,1,0:T(8,128)(2,1)} fusion(bf16[1,1024,1024]{2,1,0:T(8,128)(2,1)} %param.22, bf16[1,1024,1024]{2,1,0:T(8,128)(2,1)} %param.21), kind=kLoop, calls=%fused_computation.71 | loop fusion | flops 4194304 | bytes 6291456 | tf_op jit(solution)/shard_map/convert_element_type | solution.py:147
  102.0 2.8 gather_fusion.1
  105.3 6.9 %all-to-all-start.1 = ((bf16[4,2,2,128,1024]{4,3,2,1,0:T(8,128)(2,1)}), bf16[4,2,2,128,1024]{4,3,2,1,0:T(8,128)(2,1)}, u32[]{:S(2)}, u32[]{:S(2)}) async-start(bf16[4,2,2,128,1024]{4,3,2,1,0:T(8,128)(2,1)} %bitcast.159), calls=%async_computation.1 | async-start | bytes 8388608 | tf_op jit(solution)/shard_map/all_to_all | solution.py:126
  113.8 1.3 copy.57
  116.4 159.2 %broadcast_select_fusion = f32[8,144,1024]{2,0,1:T(8,128)S(1)} fusion(pred[8,144]{0,1:T(8,128)(4,1)S(1)} %copy-done.16, bf16[128,1,1024]{2,0,1:T(8,128)(2,1)S(1)} %bitcast.165, bf16[8,271,1024]{2,0,1:T(8,128)(2,1)S(1)} %fusion.70), kind=kOutput, calls=%fused_computation.73 | convolution fusion | flops 303169536 | bytes 9421952 | tf_op jit(solution)/shard_map/slice | solution.py:150
  275.7 2.7 copy.59
  278.4 1.8 fusion.47
  280.3 51.4 %while.29 = (s32[]{:T(128)}, f32[8,1024]{1,0:T(8,128)S(1)}, f32[8,1024]{1,0:T(8,128)S(1)}, f32[8,1024,128]{2,1,0:T(8,128)}, pred[4,2]{1,0:T(4,128)(4,1)S(1)}, /*...) while((s32[]{:T(128)}, f32[8,1024]{1,0:T(8,128)S(1)}, ...), condition=%wide.region_10.12_spmd, body=%wide.region_7.11_spmd.sunk | while | flops 1103118336 | bytes 77071520 | solution.py:145
  280.4 1.3 copy_bitcast_fusion.7
  281.8 1.4 bitcast_reduce_fusion.2
  283.2 2.3 fusion.87
  285.7 5.5 %multiply_add_fusion.5 = f32[8,1024,128]{2,1,0:T(8,128)S(1)} fusion(f32[8,1024,128]{2,1,0:T(8,128)S(1)} %copy-done.10, f32[8,1024]{1,0:T(8,128)S(1)} %get-tuple-element.315, f32[8,256,1024]{2,1,0:T(8,128)S(1)} %get-tuple-element.313, f32[8,1024]{1,0:T(8,128)S(1)} %max.10, pred[256]{0:T(512)(128)(4,1)S(1)} %broadcast_bitcast_fusion.2, ...), kind=kOutput, calls=%fused_computation.13.clone.1 | convolution fusion | flops 549453824 | bytes 17367296 | tf_op jit(solution)/shard_map/while/body/eval_jaxpr/hqk,khd->hqd/dot_general | solution.py:34
  291.2 1.9 copy-done.11
  294.7 1.4 bitcast_reduce_fusion.2
  296.1 2.3 fusion.87
  298.6 5.5 %multiply_add_fusion.5 = f32[8,1024,128]{2,1,0:T(8,128)S(1)} fusion(f32[8,1024,128]{2,1,0:T(8,128)S(1)} %copy-done.10, f32[8,1024]{1,0:T(8,128)S(1)} %get-tuple-element.315, f32[8,256,1024]{2,1,0:T(8,128)S(1)} %get-tuple-element.313, f32[8,1024]{1,0:T(8,128)S(1)} %max.10, pred[256]{0:T(512)(128)(4,1)S(1)} %broadcast_bitcast_fusion.2, ...), kind=kOutput, calls=%fused_computation.13.clone.1 | convolution fusion | flops 549453824 | bytes 17367296 | tf_op jit(solution)/shard_map/while/body/eval_jaxpr/hqk,khd->hqd/dot_general | solution.py:34
  304.1 1.9 copy-done.11
  307.5 1.4 bitcast_reduce_fusion.2
  309.0 2.3 fusion.87
  311.4 5.5 %multiply_add_fusion.5 = f32[8,1024,128]{2,1,0:T(8,128)S(1)} fusion(f32[8,1024,128]{2,1,0:T(8,128)S(1)} %copy-done.10, f32[8,1024]{1,0:T(8,128)S(1)} %get-tuple-element.315, f32[8,256,1024]{2,1,0:T(8,128)S(1)} %get-tuple-element.313, f32[8,1024]{1,0:T(8,128)S(1)} %max.10, pred[256]{0:T(512)(128)(4,1)S(1)} %broadcast_bitcast_fusion.2, ...), kind=kOutput, calls=%fused_computation.13.clone.1 | convolution fusion | flops 549453824 | bytes 17367296 | tf_op jit(solution)/shard_map/while/body/eval_jaxpr/hqk,khd->hqd/dot_general | solution.py:34
  316.9 1.9 copy-done.11
  320.4 1.4 bitcast_reduce_fusion.2
  321.8 2.3 fusion.87
  324.3 5.5 %multiply_add_fusion.5 = f32[8,1024,128]{2,1,0:T(8,128)S(1)} fusion(f32[8,1024,128]{2,1,0:T(8,128)S(1)} %copy-done.10, f32[8,1024]{1,0:T(8,128)S(1)} %get-tuple-element.315, f32[8,256,1024]{2,1,0:T(8,128)S(1)} %get-tuple-element.313, f32[8,1024]{1,0:T(8,128)S(1)} %max.10, pred[256]{0:T(512)(128)(4,1)S(1)} %broadcast_bitcast_fusion.2, ...), kind=kOutput, calls=%fused_computation.13.clone.1 | convolution fusion | flops 549453824 | bytes 17367296 | tf_op jit(solution)/shard_map/while/body/eval_jaxpr/hqk,khd->hqd/dot_general | solution.py:34
  329.8 1.9 copy-done.11
  331.7 2.9 divide_bitcast_fusion
  334.6 2.7 copy.67
  337.3 4.2 %reshape.131 = bf16[1,1024,1024]{2,1,0:T(8,128)(2,1)} reshape(bf16[1024,8,128]{2,1,0:T(8,128)(2,1)} %copy.67) | data formatting | bytes 4194304 | tf_op jit(solution)/shard_map/reshape | solution.py:156
  341.4 3.3 select_convert_fusion
  (134 shorter events, 17.0 us)
Async XLA Ops:
  0.6 101.4 %copy-start = (bf16[4,2,128,1024]{3,2,1,0:T(8,128)(2,1)S(1)}, bf16[4,2,128,1024]{3,2,1,0:T(8,128)(2,1)}, u32[]{:S(2)}) copy-start(bf16[4,2,128,1024]{3,2,1,0:T(8,128)(2,1)} %param.29) | copy-start | bytes 6291460
  0.6 12.2 %copy-start.15 = (s32[4]{0:T(128)S(1)}, s32[4]{0:T(128)}, u32[]{:S(2)}) copy-start(s32[4]{0:T(128)} %param.32) | copy-start | bytes 52
  0.7 12.2 %copy-start.4 = (s32[4,8]{1,0:T(4,128)S(1)}, s32[4,8]{1,0:T(4,128)}, u32[]{:S(2)}) copy-start(s32[4,8]{1,0:T(4,128)} %param.30) | copy-start | bytes 388
  0.7 97.9 %collective-permute-start = (bf16[1024,32]{0,1:T(8,128)(2,1)}, bf16[1024,32]{0,1:T(8,128)(2,1)S(1)}, u32[]{:S(2)}, u32[]{:S(2)}) collective-permute-start(bf16[1024,32]{0,1:T(8,128)(2,1)} %param.23), channel_id=1, source_target_pairs={{0,4},{4,0},{8,12},{12,8},{1,5},{5,1},{9,13},{13,9},{2,6},{6,2},{1... | collective-permute-start | bytes 196616 | tf_op jit(solution)/shard_map/ppermute | solution.py:72
  8.3 97.0 %all-to-all-start = ((bf16[4,128,1024]{2,1,0:T(8,128)(2,1)}), bf16[4,128,1024]{2,1,0:T(8,128)(2,1)}, u32[]{:S(2)}, u32[]{:S(2)}) async-start(bf16[4,128,1024]{2,1,0:T(8,128)(2,1)} %gather_fusion), calls=%async_computation | async-start | bytes 2097152 | tf_op jit(solution)/shard_map/all_to_all | solution.py:41
  28.4 65.1 %copy-start.5 = (s32[4,8]{1,0:T(4,128)S(1)}, s32[4,8]{1,0:T(4,128)}, u32[]{:S(2)}) copy-start(s32[4,8]{1,0:T(4,128)} %param.31) | copy-start | bytes 388
  28.4 4.3 %copy-start.2 = (bf16[1024,8,128]{2,0,1:T(8,128)(2,1)S(1)}, bf16[1024,8,128]{2,0,1:T(8,128)(2,1)}, u32[]{:S(2)}) copy-start(bf16[1024,8,128]{2,0,1:T(8,128)(2,1)} %get-tuple-element.357) | copy-start | bytes 6291460 | tf_op jit(solution)/shard_map/while
  40.2 8.6 %copy-start.6 = (bf16[1,512,8,128]{3,2,1,0:T(8,128)(2,1)S(1)}, bf16[1,512,8,128]{3,2,1,0:T(8,128)(2,1)}, u32[]{:S(2)}) copy-start(bf16[1,512,8,128]{3,2,1,0:T(8,128)(2,1)} %get-tuple-element.330) | copy-start | bytes 3145732 | tf_op jit(solution)/shard_map/while
  40.2 8.6 %copy-start.8 = (f32[8,1024,128]{2,1,0:T(8,128)S(1)}, f32[8,1024,128]{2,1,0:T(8,128)}, u32[]{:S(2)}) copy-start(f32[8,1024,128]{2,1,0:T(8,128)} %get-tuple-element.344) | copy-start | bytes 12582916 | tf_op jit(solution)/shard_map/while
  58.6 1.9 copy-start.9
  60.6 4.3 %copy-start.2 = (bf16[1024,8,128]{2,0,1:T(8,128)(2,1)S(1)}, bf16[1024,8,128]{2,0,1:T(8,128)(2,1)}, u32[]{:S(2)}) copy-start(bf16[1024,8,128]{2,0,1:T(8,128)(2,1)} %get-tuple-element.357) | copy-start | bytes 6291460 | tf_op jit(solution)/shard_map/while
  72.3 8.6 %copy-start.6 = (bf16[1,512,8,128]{3,2,1,0:T(8,128)(2,1)S(1)}, bf16[1,512,8,128]{3,2,1,0:T(8,128)(2,1)}, u32[]{:S(2)}) copy-start(bf16[1,512,8,128]{3,2,1,0:T(8,128)(2,1)} %get-tuple-element.330) | copy-start | bytes 3145732 | tf_op jit(solution)/shard_map/while
  72.3 8.6 %copy-start.8 = (f32[8,1024,128]{2,1,0:T(8,128)S(1)}, f32[8,1024,128]{2,1,0:T(8,128)}, u32[]{:S(2)}) copy-start(f32[8,1024,128]{2,1,0:T(8,128)} %get-tuple-element.344) | copy-start | bytes 12582916 | tf_op jit(solution)/shard_map/while
  90.7 1.9 copy-start.9
  92.7 5.9 %copy-start.13 = (bf16[1024,32]{0,1:T(8,128)(2,1)S(1)}, bf16[1024,32]{0,1:T(8,128)(2,1)}, u32[]{:S(2)}) copy-start(bf16[1024,32]{0,1:T(8,128)(2,1)} %param.23) | copy-start | bytes 196612
  92.7 8.0 %copy-start.14 = (f32[1024]{0:T(1024)S(1)}, f32[1024]{0:T(1024)}, u32[]{:S(2)}) copy-start(f32[1024]{0:T(1024)} %param.24) | copy-start | bytes 12292
  98.6 6.2 %collective-permute-start.1 = (bf16[1024,64]{0,1:T(8,128)(2,1)S(1)}, bf16[1024,64]{0,1:T(8,128)(2,1)S(1)}, u32[]{:S(2)}, u32[]{:S(2)}) collective-permute-start(bf16[1024,64]{0,1:T(8,128)(2,1)S(1)} %maximum_select_fusion.1), channel_id=1, source_target_pairs={{0,8},{4,12},{8,0},{12,4},{1,9},{5,13},{9,1},{13,5},{2,10},{6,14},... | collective-permute-start | bytes 393224 | tf_op jit(solution)/shard_map/ppermute | solution.py:72
  105.3 7.9 %copy-start.7 = (bf16[1,1024,1024]{2,1,0:T(8,128)(2,1)S(1)}, bf16[1,1024,1024]{2,1,0:T(8,128)(2,1)}, u32[]{:S(2)}) copy-start(bf16[1,1024,1024]{2,1,0:T(8,128)(2,1)} %multiply_convert_fusion) | copy-start | bytes 6291460
  105.3 175.0 %all-to-all-start.1 = ((bf16[4,2,2,128,1024]{4,3,2,1,0:T(8,128)(2,1)}), bf16[4,2,2,128,1024]{4,3,2,1,0:T(8,128)(2,1)}, u32[]{:S(2)}, u32[]{:S(2)}) async-start(bf16[4,2,2,128,1024]{4,3,2,1,0:T(8,128)(2,1)} %bitcast.159), calls=%async_computation.1 | async-start | bytes 8388608 | tf_op jit(solution)/shard_map/all_to_all | solution.py:126
  115.6 0.8 copy-start.16
  275.6 2.8 copy-start.12
  278.4 1.9 copy-start.3
  283.2 2.5 copy-start.10
  291.2 1.9 copy-start.11
  296.1 2.5 copy-start.10
  304.0 1.9 copy-start.11
  308.9 2.5 copy-start.10
  316.9 1.9 copy-start.11
  321.8 2.5 copy-start.10
  329.8 1.9 copy-start.11
  334.6 10.2 %copy-start.1 = (bf16[4,2,128,1024]{3,2,1,0:T(8,128)(2,1)S(1)}, bf16[4,2,128,1024]{3,2,1,0:T(8,128)(2,1)}, u32[]{:S(2)}) copy-start(bf16[4,2,128,1024]{3,2,1,0:T(8,128)(2,1)} %param.29) | copy-start | bytes 6291460
